TPU v7x, 512 devices: a whole 4x8x8 slice. The times are simulated.
512 devices in a mesh: head: 8 (over y_lo, x), seq: 64 (over y_hi, z, core).
Axes of the slice: x: 4, y: 8 (y_hi: 4, y_lo: 2; y = y_hi * 2 + y_lo), z: 8, core: 2. Of those that a mesh axis runs over, the one named last changes fastest.
Arguments:
- queries: bfloat16 [2, 4096, 4096], P(None, 'seq', 'head'), may hold values from -256 to 256
- keys: bfloat16 [2, 4096, 4096], P(None, 'seq', 'head'), may hold values from -256 to 256
- values: bfloat16 [2, 4096, 4096], P(None, 'seq', 'head'), may hold values from -6 to 6
- token_rates: float32 [1, 16, 4096], P(None, 'head', 'seq'), may hold values from 0.1 to 1
- step_size: float32 [16], P('head'), may hold values from 0.3 to 1
- w_gate: bfloat16 [16, 256, 512], P('head', 'seq'), may hold values from -0.375 to 0.375
- w_up: bfloat16 [16, 256, 512], P('head', 'seq'), may hold values from -0.375 to 0.375
- w_down: bfloat16 [16, 512, 256], P('head', 'seq'), may hold values from -0.25 to 0.25
- norm_gain: float32 [4096], replicated, may hold values from 0.5 to 1.5
Outputs:
- mixed: bfloat16 [2, 4096, 4096], P(None, ('seq', 'head'))
All inputs are finite; a program needn't handle non-finite values.
Results may differ from a plain program's by a relative error of at most 0.0095.
Values may be sent and summed in bfloat16 or wider, within the bound.
No kernel may reach another device: no remote copies, remote signals or barrier semaphores. Data moves between devices by JAX's collectives and lax.ppermute only.
A program may use at most 64 MiB of HBM per device.

v0:
```python
import math
import jax
import jax.numpy as jnp
from jax import lax
from jax.sharding import PartitionSpec as P

DH = 256
DF = 512
WIN = 512
NS_STEPS = 5


def spread(block, axis, holder):
    block = jnp.where(lax.axis_index(axis) == holder, block, jnp.zeros_like(block))
    return lax.psum(block, axis)


def shifted(array, axis, by):
    count = lax.axis_size(axis)
    return lax.ppermute(array, axis, [(i, (i + by) % count) for i in range(count)])


def rms_norm(values_in):
    wide = values_in.astype(jnp.float32)
    mean_square = jnp.mean(wide * wide, axis=-1, keepdims=True)
    return (wide * lax.rsqrt(mean_square + 1e-06)).astype(jnp.bfloat16)


def newton(grad_in):
    norm_value = jnp.sqrt(jnp.sum(grad_in * grad_in))
    iterate = grad_in / (norm_value + 1e-07)
    for _ in range(NS_STEPS):
        gram = jnp.dot(
            iterate, iterate.T, precision=lax.Precision.HIGHEST, preferred_element_type=jnp.float32
        )
        poly = -4.775 * gram + 2.0315 * jnp.dot(
            gram, gram, precision=lax.Precision.HIGHEST, preferred_element_type=jnp.float32
        )
        iterate = 3.4445 * iterate + jnp.dot(
            poly, iterate, precision=lax.Precision.HIGHEST, preferred_element_type=jnp.float32
        )
    return iterate


def orthogonalize(summed, seq_count, seq_index):
    problems = summed.shape[0]
    stride = 1
    problem = jnp.clip(seq_index // stride + 0, 0, problems - 1)
    owned = [newton(lax.dynamic_index_in_dim(summed, problem, 0, keepdims=False))]
    results = []
    for problem_index in range(problems):
        results.append(
            spread(
                owned[problem_index // seq_count].astype(jnp.bfloat16),
                "seq",
                problem_index % seq_count * stride,
            ).astype(jnp.float32)
        )
    return jnp.stack(results)


def body(queries, keys, values, token_rates, step_size, w_gate, w_up, w_down, norm_gain):
    blocks_here, tok_rows, width_here = queries.shape
    head_count = width_here // DH
    seq_count = lax.axis_size("seq")
    seq_index = lax.axis_index("seq")
    gate_fast, up_fast, down_fast = (
        lax.all_gather(w_gate, "seq", axis=1, tiled=True),
        lax.all_gather(w_up, "seq", axis=1, tiled=True),
        lax.all_gather(w_down, "seq", axis=1, tiled=True),
    )
    reach_count = -(-WIN // tok_rows)
    earlier_blocks = []
    for distance in range(1, reach_count + 1):
        arrived = shifted((keys, values), "seq", distance)
        settled = []
        for part_arr in arrived:
            before = jnp.concatenate([jnp.zeros_like(part_arr[:1]), part_arr[:-1]], 0)
            settled.append(jnp.where(seq_index >= distance, part_arr, before))
        earlier_blocks.insert(0, settled)
    context_keys = jnp.concatenate([pair_item[0] for pair_item in earlier_blocks] + [keys], 1)
    context_values = jnp.concatenate([pair_item[1] for pair_item in earlier_blocks] + [values], 1)
    context_len = context_keys.shape[1]
    context_keys = context_keys.reshape(blocks_here, context_len, head_count, DH)
    context_values = context_values.reshape(blocks_here, context_len, head_count, DH)
    query_heads = queries.reshape(blocks_here, tok_rows, head_count, DH)
    key_heads = keys.reshape(blocks_here, tok_rows, head_count, DH)
    value_heads = values.reshape(blocks_here, tok_rows, head_count, DH)
    scores = jnp.einsum(
        "bihd,bjhd->bhij", query_heads, context_keys, preferred_element_type=jnp.float32
    ) * (1.0 / math.sqrt(DH))
    query_rows = jnp.arange(tok_rows, dtype=jnp.int32)
    key_rows = jnp.arange(context_len, dtype=jnp.int32)
    row_gap = reach_count * tok_rows + query_rows[:, None] - key_rows[None, :]
    block_ids = jnp.arange(blocks_here, dtype=jnp.int32)
    key_pos = (
        block_ids[:, None] * (tok_rows * seq_count)
        + seq_index * tok_rows
        - reach_count * tok_rows
        + key_rows[None, :]
    )
    allowed = ((row_gap >= 0) & (row_gap < WIN))[None, :, :] & (key_pos >= 0)[:, None, :]
    scores = jnp.where(allowed[:, None, :, :], scores, -1e30)
    row_top = jnp.max(scores, axis=-1, keepdims=True)
    exp_scores = jnp.exp(scores - row_top)
    attn_weights = (exp_scores / jnp.sum(exp_scores, axis=-1, keepdims=True)).astype(jnp.bfloat16)
    attention = jnp.einsum(
        "bhij,bjhd->bihd", attn_weights, context_values, preferred_element_type=jnp.float32
    )
    query_norm = rms_norm(query_heads)
    key_norm = rms_norm(key_heads[: blocks_here - 1])
    fast_parts = []
    for block_index in range(blocks_here):
        gate_query = jnp.einsum(
            "thd,hdf->htf", query_norm[block_index], gate_fast, preferred_element_type=jnp.float32
        )
        up_query = jnp.einsum(
            "thd,hdf->htf", query_norm[block_index], up_fast, preferred_element_type=jnp.float32
        )
        hidden = (jax.nn.silu(gate_query) * up_query).astype(jnp.bfloat16)
        fast_parts.append(
            jnp.einsum("htf,hfd->thd", hidden, down_fast, preferred_element_type=jnp.float32)
        )
        if block_index < blocks_here - 1:
            keys_now = key_norm[block_index]
            vals_now = value_heads[block_index]
            gate_pre = jnp.einsum(
                "thd,hdf->htf", keys_now, gate_fast, preferred_element_type=jnp.float32
            )
            up_pre = jnp.einsum(
                "thd,hdf->htf", keys_now, up_fast, preferred_element_type=jnp.float32
            )
            back = jnp.einsum(
                "thd,hfd->htf", vals_now, down_fast, preferred_element_type=jnp.float32
            )
            rate_col = token_rates[block_index][:, :, None]
            sigmoid_val = jax.nn.sigmoid(gate_pre)
            act_val = gate_pre * sigmoid_val
            d_gate = (
                rate_col * back * up_pre * sigmoid_val * (1.0 + gate_pre * (1.0 - sigmoid_val))
            ).astype(jnp.bfloat16)
            d_up = (rate_col * back * act_val).astype(jnp.bfloat16)
            h_rate = (rate_col * act_val * up_pre).astype(jnp.bfloat16)
            grad_gate = jnp.einsum(
                "thd,htf->hdf", keys_now, d_gate, preferred_element_type=jnp.float32
            )
            grad_up = jnp.einsum("thd,htf->hdf", keys_now, d_up, preferred_element_type=jnp.float32)
            grad_down_t = jnp.einsum(
                "thd,htf->hdf", vals_now, h_rate, preferred_element_type=jnp.float32
            )
            stacked = jnp.stack([grad_gate, grad_up, grad_down_t], 1).reshape(
                head_count * 3, DH, DF
            )
            summed = lax.psum(stacked, "seq")
            orthogonal = orthogonalize(summed, seq_count, seq_index).reshape(head_count, 3, DH, DF)
            step_col = step_size[:, None, None]
            gate_fast = (gate_fast.astype(jnp.float32) + step_col * orthogonal[:, 0]).astype(
                jnp.bfloat16
            )
            up_fast = (up_fast.astype(jnp.float32) + step_col * orthogonal[:, 1]).astype(
                jnp.bfloat16
            )
            down_fast = (
                down_fast.astype(jnp.float32) + step_col * jnp.swapaxes(orthogonal[:, 2], 1, 2)
            ).astype(jnp.bfloat16)
    fast_out = jnp.stack(fast_parts)
    combined = (
        (fast_out + attention).astype(jnp.bfloat16).reshape(blocks_here, tok_rows, width_here)
    )
    wide = lax.all_to_all(combined, "head", split_axis=1, concat_axis=2, tiled=True).astype(
        jnp.float32
    )
    mean_square = jnp.mean(wide * wide, axis=-1, keepdims=True)
    return (wide * lax.rsqrt(mean_square + 1e-06) * norm_gain).astype(jnp.bfloat16)


def solution(mesh):
    placed = (
        P(None, "seq", "head"),
        P(None, "seq", "head"),
        P(None, "seq", "head"),
        P(None, "head", "seq"),
        P("head"),
        P("head", "seq", None),
        P("head", "seq", None),
        P("head", "seq", None),
        P(),
    )
    return jax.shard_map(
        body, mesh=mesh, in_specs=placed, out_specs=P(None, ("seq", "head"), None), check_vma=False
    )
```

profile of v0, /device:TPU:1, one launch (start us, length us, event | category | flops | bytes accessed | tf_op | source)
XLA Modules:
  0.0 1475.3 jit_solution(10621219490444785268)
XLA Ops:
  6.5 11.6 collective-permute-start
  18.1 2.5 collective-permute-start.1
  20.6 6.6 collective-permute-start.2
  27.2 5.8 collective-permute-start.3
  33.0 4.0 collective-permute-start.4
  37.1 0.9 fusion.87
  37.9 0.9 slice_convert_fusion
  38.8 0.8 slice.75
  40.1 88.6 %all_gather.9 = bf16[2,256,512]{2,0,1:T(2,128)(2,1)S(1)} all-gather(bf16[2,4,512]{2,0,1:T(2,128)(2,1)S(1)} %copy.91), channel_id=1, replica_groups=mesh['head'=8,'seq'=64] {'seq'}, dimensions={1}, use_global_device_ids=true | all-gather | bytes 532480 | tf_op jit(solution)/shard_map/all_gather | solution.py:68
  128.6 80.5 %all_gather.10 = bf16[2,256,512]{2,0,1:T(2,128)(2,1)S(1)} all-gather(bf16[2,4,512]{2,0,1:T(2,128)(2,1)S(1)} %copy.93), channel_id=1, replica_groups=mesh['head'=8,'seq'=64] {'seq'}, dimensions={1}, use_global_device_ids=true | all-gather | bytes 532480 | tf_op jit(solution)/shard_map/all_gather | solution.py:69
  209.7 77.9 %all_gather.11 = bf16[2,512,256]{2,0,1:T(2,128)(2,1)S(1)} all-gather(bf16[2,8,256]{2,0,1:T(2,128)(2,1)S(1)} %copy.95), channel_id=1, replica_groups=mesh['head'=8,'seq'=64] {'seq'}, dimensions={1}, use_global_device_ids=true | all-gather | bytes 532480 | tf_op jit(solution)/shard_map/all_gather | solution.py:70
  290.2 2.0 copy.106
  293.3 0.9 fusion.57
  294.4 1.9 collective-permute-start.5
  296.5 3.4 collective-permute-start.6
  299.9 1.9 collective-permute-start.8
  301.9 1.9 collective-permute-start.9
  303.8 4.7 collective-permute-start.10
  308.5 11.1 collective-permute-start.11
  319.7 3.0 collective-permute-start.12
  322.8 2.7 collective-permute-start.13
  325.5 3.4 collective-permute-done.9
  328.9 1.9 collective-permute-start.14
  330.8 5.3 collective-permute-done.10
  336.1 1.9 collective-permute-start.15
  338.0 2.3 collective-permute-done.11
  340.3 5.9 collective-permute-start.7
  346.3 2.0 convolution_bitcast_fusion.4
  348.4 1.0 slice.102
  349.5 0.9 slice.105
  351.2 9.3 collective-permute-done.14
  360.5 0.9 slice.108
  366.0 1.0 copy-done.34
  367.7 503.6 %all-reduce.20.cloned.1.call-done = f32[6,256,512]{2,1,0:T(8,128)} async-done(((f32[6,256,512]{2,1,0:T(8,128)}), f32[6,256,512]{2,1,0:T(8,128)}) %all-reduce.20.cloned.1.call-update) | async-done | bytes 3145744 | tf_op jit(solution)/shard_map/psum | solution.py:154
  871.3 1.8 multiply_reduce_fusion
  873.8 1.8 fusion.43
  876.0 1.9 convolution_add_fusion.4
  883.9 1.9 select_bitcast_fusion
  885.8 0.8 copy-done.18
  888.7 1.7 select_dynamic-update-slice_fusion
  891.8 1.7 fusion.4
  893.8 555.3 %all-reduce.22.cloned.1.call-done = (bf16[1,256,512]{2,1,0:T(8,128)(2,1)}, bf16[1,256,512]{2,1,0:T(8,128)(2,1)}, bf16[1,256,512]{2,1,0:T(8,128)(2,1)}, bf16[1,25...) async-done(((bf16[1,256,512]{2,1,0:T(8,128)(2,1)}, bf16[1,256,512]{2,1,0:T(8,128)(2,1)}, bf16[1,256,512]{2,1,0:T(8,128)(2,1)}, ...) | async-done | bytes 1572880 | tf_op jit(solution)/shard_map/psum | solution.py:15
  1449.1 1.0 constant_dynamic-update-slice_fusion.5
  1450.2 1.0 constant_dynamic-update-slice_fusion.4
  1451.8 1.7 copy-done
  1453.8 2.1 convolution_bitcast_fusion.3
  1455.9 1.8 fusion.24
  1457.9 9.3 all_to_all.4
  (190 shorter events, 23.2 us)
Async XLA Ops:
  6.5 33.5 %copy-start.35 = (bf16[2,4,512]{2,1,0:T(4,128)(2,1)S(1)}, bf16[2,4,512]{2,1,0:T(4,128)(2,1)}, u32[]{:S(2)}) copy-start(bf16[2,4,512]{2,1,0:T(4,128)(2,1)} %param.14) | copy-start | bytes 24580
  6.5 122.1 %copy-start.36 = (bf16[2,4,512]{2,1,0:T(4,128)(2,1)S(1)}, bf16[2,4,512]{2,1,0:T(4,128)(2,1)}, u32[]{:S(2)}) copy-start(bf16[2,4,512]{2,1,0:T(4,128)(2,1)} %param.15) | copy-start | bytes 24580
  6.5 864.8 %all-reduce.20.cloned.1.call-start = ((), (), s32[]{:S(2)}) async-start(), calls=%async_computation.1 | async-start | bytes 6291456 | tf_op jit(solution)/shard_map/psum | solution.py:154
  6.5 287.9 %collective-permute-start = (bf16[2,64,512]{2,1,0:T(8,128)(2,1)}, bf16[2,64,512]{2,1,0:T(8,128)(2,1)S(1)}, u32[]{:S(2)}, u32[]{:S(2)}) collective-permute-start(bf16[2,64,512]{2,1,0:T(8,128)(2,1)} %param.11), channel_id=1, source_target_pairs={{0,8},{1,9},{2,10},{3,11},{4,12},{5,13},{6,14},{7,15},{8,16},{9,17... | collective-permute-start | bytes 393224 | tf_op jit(solution)/shard_map/ppermute | solution.py:20
  18.1 278.3 %collective-permute-start.1 = (bf16[2,64,512]{2,1,0:T(8,128)(2,1)}, bf16[2,64,512]{2,1,0:T(8,128)(2,1)S(1)}, u32[]{:S(2)}, u32[]{:S(2)}) collective-permute-start(bf16[2,64,512]{2,1,0:T(8,128)(2,1)} %param.11), channel_id=1, source_target_pairs={{0,7},{1,8},{2,9},{3,10},{4,11},{5,12},{6,13},{7,14},{8,15},{9,16}... | collective-permute-start | bytes 393224 | tf_op jit(solution)/shard_map/ppermute | solution.py:20
  20.6 279.3 %collective-permute-start.2 = (bf16[2,64,512]{2,1,0:T(8,128)(2,1)}, bf16[2,64,512]{2,1,0:T(8,128)(2,1)S(1)}, u32[]{:S(2)}, u32[]{:S(2)}) collective-permute-start(bf16[2,64,512]{2,1,0:T(8,128)(2,1)} %param.11), channel_id=1, source_target_pairs={{0,6},{1,7},{2,8},{3,9},{4,10},{5,11},{6,12},{7,13},{8,14},{9,15},... | collective-permute-start | bytes 393224 | tf_op jit(solution)/shard_map/ppermute | solution.py:20
  27.2 274.7 %collective-permute-start.3 = (bf16[2,64,512]{2,1,0:T(8,128)(2,1)}, bf16[2,64,512]{2,1,0:T(8,128)(2,1)S(1)}, u32[]{:S(2)}, u32[]{:S(2)}) collective-permute-start(bf16[2,64,512]{2,1,0:T(8,128)(2,1)} %param.11), channel_id=1, source_target_pairs={{0,5},{1,6},{2,7},{3,8},{4,9},{5,10},{6,11},{7,12},{8,13},{9,14},{... | collective-permute-start | bytes 393224 | tf_op jit(solution)/shard_map/ppermute | solution.py:20
  33.0 270.8 %collective-permute-start.4 = (bf16[2,64,512]{2,1,0:T(8,128)(2,1)}, bf16[2,64,512]{2,1,0:T(8,128)(2,1)S(1)}, u32[]{:S(2)}, u32[]{:S(2)}) collective-permute-start(bf16[2,64,512]{2,1,0:T(8,128)(2,1)} %param.11), channel_id=1, source_target_pairs={{0,4},{1,5},{2,6},{3,7},{4,8},{5,9},{6,10},{7,11},{8,12},{9,13},{1... | collective-permute-start | bytes 393224 | tf_op jit(solution)/shard_map/ppermute | solution.py:20
  128.6 81.0 %copy-start.37 = (bf16[2,8,256]{2,1,0:T(8,128)(2,1)S(1)}, bf16[2,8,256]{2,1,0:T(8,128)(2,1)}, u32[]{:S(2)}) copy-start(bf16[2,8,256]{2,1,0:T(8,128)(2,1)} %param.16) | copy-start | bytes 24580
  209.4 78.9 %copy-start.38 = (f32[1,2,64]{2,1,0:T(2,128)S(1)}, f32[1,2,64]{2,1,0:T(2,128)}, u32[]{:S(2)}) copy-start(f32[1,2,64]{2,1,0:T(2,128)} %param.12) | copy-start | bytes 1540
  292.2 7.7 copy-start.1
  292.2 1156.9 %all-reduce.22.cloned.1.call-start = ((), (), s32[]{:S(2)}) async-start(), calls=%async_computation.2 | async-start | bytes 3145728 | tf_op jit(solution)/shard_map/psum | solution.py:15
  294.4 53.9 %copy-start.11 = (bf16[2,64,512]{2,1,0:T(8,128)(2,1)}, bf16[2,64,512]{2,1,0:T(8,128)(2,1)S(1)}, u32[]{:S(2)}) copy-start(bf16[2,64,512]{2,1,0:T(8,128)(2,1)S(1)} %collective-permute-done) | copy-start | bytes 393220
  294.4 14.1 collective-permute-start.5
  296.4 51.9 %copy-start.9 = (bf16[2,64,512]{2,1,0:T(8,128)(2,1)}, bf16[2,64,512]{2,1,0:T(8,128)(2,1)S(1)}, u32[]{:S(2)}) copy-start(bf16[2,64,512]{2,1,0:T(8,128)(2,1)S(1)} %collective-permute-done.1) | copy-start | bytes 393220
  296.5 23.2 %collective-permute-start.6 = (bf16[2,64,512]{2,1,0:T(8,128)(2,1)S(1)}, bf16[2,64,512]{2,1,0:T(8,128)(2,1)S(1)}, u32[]{:S(2)}, u32[]{:S(2)}) collective-permute-start(bf16[2,64,512]{2,1,0:T(8,128)(2,1)S(1)} %copy-done.27), channel_id=1, source_target_pairs={{0,2},{1,3},{2,4},{3,5},{4,6},{5,7},{6,8},{7,9},{8,10},{9,11},{10,... | collective-permute-start | bytes 393224 | tf_op jit(solution)/shard_map/ppermute | solution.py:20
  299.9 48.4 %copy-start.7 = (bf16[2,64,512]{2,1,0:T(8,128)(2,1)}, bf16[2,64,512]{2,1,0:T(8,128)(2,1)S(1)}, u32[]{:S(2)}) copy-start(bf16[2,64,512]{2,1,0:T(8,128)(2,1)S(1)} %collective-permute-done.2) | copy-start | bytes 393220
  299.9 22.8 %collective-permute-start.8 = (bf16[2,64,512]{2,1,0:T(8,128)(2,1)S(1)}, bf16[2,64,512]{2,1,0:T(8,128)(2,1)S(1)}, u32[]{:S(2)}, u32[]{:S(2)}) collective-permute-start(bf16[2,64,512]{2,1,0:T(8,128)(2,1)S(1)} %copy-done.1), channel_id=1, source_target_pairs={{0,8},{1,9},{2,10},{3,11},{4,12},{5,13},{6,14},{7,15},{8,16},{9,17... | collective-permute-start | bytes 393224 | tf_op jit(solution)/shard_map/ppermute | solution.py:20
  301.9 46.5 %copy-start.5 = (bf16[2,64,512]{2,1,0:T(8,128)(2,1)}, bf16[2,64,512]{2,1,0:T(8,128)(2,1)S(1)}, u32[]{:S(2)}) copy-start(bf16[2,64,512]{2,1,0:T(8,128)(2,1)S(1)} %collective-permute-done.3) | copy-start | bytes 393220
  301.9 27.0 %collective-permute-start.9 = (bf16[2,64,512]{2,1,0:T(8,128)(2,1)S(1)}, bf16[2,64,512]{2,1,0:T(8,128)(2,1)}, u32[]{:S(2)}, u32[]{:S(2)}) collective-permute-start(bf16[2,64,512]{2,1,0:T(8,128)(2,1)S(1)} %copy-done.1), channel_id=1, source_target_pairs={{0,7},{1,8},{2,9},{3,10},{4,11},{5,12},{6,13},{7,14},{8,15},{9,16}... | collective-permute-start | bytes 393224 | tf_op jit(solution)/shard_map/ppermute | solution.py:20
  303.8 44.6 %copy-start.3 = (bf16[2,64,512]{2,1,0:T(8,128)(2,1)}, bf16[2,64,512]{2,1,0:T(8,128)(2,1)S(1)}, u32[]{:S(2)}) copy-start(bf16[2,64,512]{2,1,0:T(8,128)(2,1)S(1)} %collective-permute-done.4) | copy-start | bytes 393220
  303.8 32.2 %collective-permute-start.10 = (bf16[2,64,512]{2,1,0:T(8,128)(2,1)S(1)}, bf16[2,64,512]{2,1,0:T(8,128)(2,1)S(1)}, u32[]{:S(2)}, u32[]{:S(2)}) collective-permute-start(bf16[2,64,512]{2,1,0:T(8,128)(2,1)S(1)} %copy-done.1), channel_id=1, source_target_pairs={{0,6},{1,7},{2,8},{3,9},{4,10},{5,11},{6,12},{7,13},{8,14},{9,15},... | collective-permute-start | bytes 393224 | tf_op jit(solution)/shard_map/ppermute | solution.py:20
  308.5 39.9 %copy-start.19 = (bf16[2,64,512]{2,1,0:T(8,128)(2,1)}, bf16[2,64,512]{2,1,0:T(8,128)(2,1)S(1)}, u32[]{:S(2)}) copy-start(bf16[2,64,512]{2,1,0:T(8,128)(2,1)S(1)} %collective-permute-done.5) | copy-start | bytes 393220
  308.5 31.8 %collective-permute-start.11 = (bf16[2,64,512]{2,1,0:T(8,128)(2,1)S(1)}, bf16[2,64,512]{2,1,0:T(8,128)(2,1)S(1)}, u32[]{:S(2)}, u32[]{:S(2)}) collective-permute-start(bf16[2,64,512]{2,1,0:T(8,128)(2,1)S(1)} %copy-done.1), channel_id=1, source_target_pairs={{0,5},{1,6},{2,7},{3,8},{4,9},{5,10},{6,11},{7,12},{8,13},{9,14},{... | collective-permute-start | bytes 393224 | tf_op jit(solution)/shard_map/ppermute | solution.py:20
  319.7 28.7 %copy-start.13 = (bf16[2,64,512]{2,1,0:T(8,128)(2,1)}, bf16[2,64,512]{2,1,0:T(8,128)(2,1)S(1)}, u32[]{:S(2)}) copy-start(bf16[2,64,512]{2,1,0:T(8,128)(2,1)S(1)} %collective-permute-done.6) | copy-start | bytes 393220
  319.7 29.7 %collective-permute-start.12 = (bf16[2,64,512]{2,1,0:T(8,128)(2,1)S(1)}, bf16[2,64,512]{2,1,0:T(8,128)(2,1)}, u32[]{:S(2)}, u32[]{:S(2)}) collective-permute-start(bf16[2,64,512]{2,1,0:T(8,128)(2,1)S(1)} %copy-done.1), channel_id=1, source_target_pairs={{0,4},{1,5},{2,6},{3,7},{4,8},{5,9},{6,10},{7,11},{8,12},{9,13},{1... | collective-permute-start | bytes 393224 | tf_op jit(solution)/shard_map/ppermute | solution.py:20
  322.8 28.4 %collective-permute-start.13 = (bf16[2,64,512]{2,1,0:T(8,128)(2,1)S(1)}, bf16[2,64,512]{2,1,0:T(8,128)(2,1)S(1)}, u32[]{:S(2)}, u32[]{:S(2)}) collective-permute-start(bf16[2,64,512]{2,1,0:T(8,128)(2,1)S(1)} %copy-done.1), channel_id=1, source_target_pairs={{0,3},{1,4},{2,5},{3,6},{4,7},{5,8},{6,9},{7,10},{8,11},{9,12},{10... | collective-permute-start | bytes 393224 | tf_op jit(solution)/shard_map/ppermute | solution.py:20
  328.9 31.6 %collective-permute-start.14 = (bf16[2,64,512]{2,1,0:T(8,128)(2,1)S(1)}, bf16[2,64,512]{2,1,0:T(8,128)(2,1)S(1)}, u32[]{:S(2)}, u32[]{:S(2)}) collective-permute-start(bf16[2,64,512]{2,1,0:T(8,128)(2,1)S(1)} %copy-done.1), channel_id=1, source_target_pairs={{0,2},{1,3},{2,4},{3,5},{4,6},{5,7},{6,8},{7,9},{8,10},{9,11},{10,... | collective-permute-start | bytes 393224 | tf_op jit(solution)/shard_map/ppermute | solution.py:20
  336.1 12.2 copy-start.23
  336.1 24.4 %collective-permute-start.15 = (bf16[2,64,512]{2,1,0:T(8,128)(2,1)S(1)}, bf16[2,64,512]{2,1,0:T(8,128)(2,1)}, u32[]{:S(2)}, u32[]{:S(2)}) collective-permute-start(bf16[2,64,512]{2,1,0:T(8,128)(2,1)S(1)} %copy-done.1), channel_id=1, source_target_pairs={{0,1},{1,2},{2,3},{3,4},{4,5},{5,6},{6,7},{7,8},{8,9},{9,10},{10,1... | collective-permute-start | bytes 393224 | tf_op jit(solution)/shard_map/ppermute | solution.py:20
  340.3 8.0 copy-start.21
  340.3 21.1 %collective-permute-start.7 = (bf16[2,64,512]{2,1,0:T(8,128)(2,1)}, bf16[2,64,512]{2,1,0:T(8,128)(2,1)}, u32[]{:S(2)}, u32[]{:S(2)}) collective-permute-start(bf16[2,64,512]{2,1,0:T(8,128)(2,1)} %param.11), channel_id=1, source_target_pairs={{0,1},{1,2},{2,3},{3,4},{4,5},{5,6},{6,7},{7,8},{8,9},{9,10},{10,1... | collective-permute-start | bytes 393224 | tf_op jit(solution)/shard_map/ppermute | solution.py:20
  348.3 13.9 copy-start.12
  348.3 13.9 slice-start.4
  348.3 14.6 copy-start.26
  348.3 14.6 slice-start.11
  348.4 14.6 copy-start.10
  348.4 14.6 slice-start.3
  348.4 15.3 %copy-start.8 = (bf16[2,64,512]{2,1,0:T(8,128)(2,1)S(1)}, bf16[2,64,512]{2,1,0:T(8,128)(2,1)}, u32[]{:S(2)}) copy-start(bf16[2,64,512]{2,1,0:T(8,128)(2,1)} %copy-done.7) | copy-start | bytes 393220
  348.4 15.3 %slice-start.2 = ((bf16[2,64,512]{2,1,0:T(8,128)(2,1)}), bf16[1,64,512]{2,1,0:T(8,128)(2,1)S(1)}, s32[]{:S(2)}) async-start(bf16[2,64,512]{2,1,0:T(8,128)(2,1)} %copy-done.7), calls=%async_computation.5 | async-start | bytes 131072 | tf_op jit(solution)/shard_map/slice | solution.py:78
  349.4 15.0 %copy-start.24 = (bf16[2,64,512]{2,1,0:T(8,128)(2,1)S(1)}, bf16[2,64,512]{2,1,0:T(8,128)(2,1)}, u32[]{:S(2)}) copy-start(bf16[2,64,512]{2,1,0:T(8,128)(2,1)} %copy-done.23) | copy-start | bytes 393220
  349.4 15.0 %slice-start.10 = ((bf16[2,64,512]{2,1,0:T(8,128)(2,1)}), bf16[1,64,512]{2,1,0:T(8,128)(2,1)S(1)}, s32[]{:S(2)}) async-start(bf16[2,64,512]{2,1,0:T(8,128)(2,1)} %copy-done.23), calls=%async_computation.13 | async-start | bytes 131072 | tf_op jit(solution)/shard_map/slice | solution.py:78
  351.2 13.4 copy-start.17
  351.2 13.4 copy-start.6
  351.2 13.4 slice-start.1
  360.5 4.0 copy-start.15
  886.7 4.5 copy-start.28
  1457.6 10.1 copy-start.33
  (23 other events, 46.9 us)
Sparse Core Ops, SparseCore 0:
  292.3 578.9 all-reduce.19
  885.9 563.1 all-reduce.21
where the time goes:
time: 1480 us
  waiting for transfers between devices  1080 us (73%)
  blocking collectives  256 us (17%)
  starting transfers between devices  71 us (5%)
  matrix products  22.4 us (2%)
  local copies, waits for them, and re-layouts  15.9 us (1%)
  between operations  15.2 us (1%)
    psum x1, waiting for transfers between devices, spread(): return lax.psum(block, axis)  555 us
    psum x1, waiting for transfers between devices, body(): summed = lax.psum(stacked, 'seq')  504 us
    all_gather x1, blocking collectives, body(): lax.all_gather(w_gate, 'seq', axis=1, tiled=True)  88.6 us
    all_gather x1, blocking collectives, body(): lax.all_gather(w_up, 'seq', axis=1, tiled=True)  80.5 us
    all_gather x1, blocking collectives, body(): lax.all_gather(w_down, 'seq', axis=1, tiled=True)  77.9 us
    ppermute x16, starting transfers between devices, shifted(): lax.ppermute(array, axis, [(i, (i + by) % count) for i in range(count)])  70.9 us
  transfers between devices with their start and end apart: 18, of which 7 were waited for; matrix products, arithmetic and copies ran while one was open for 2% of the time, Pallas kernels for 0%

commit v1 on v0

--- a/solution.py
+++ b/solution.py
@@ -64,10 +64,17 @@
     head_count = width_here // DH
     seq_count = lax.axis_size("seq")
     seq_index = lax.axis_index("seq")
+
+    def _turn_rails(local_x):
+        kept_rows = []
+        for _ in range(lax.axis_size("seq")):
+            kept_rows.append(local_x)
+        return jnp.concatenate(lax.all_to_all(jnp.stack(kept_rows, 0), "seq", 0, 0), 1)
+
     gate_fast, up_fast, down_fast = (
         lax.all_gather(w_gate, "seq", axis=1, tiled=True),
         lax.all_gather(w_up, "seq", axis=1, tiled=True),
-        lax.all_gather(w_down, "seq", axis=1, tiled=True),
+        _turn_rails(w_down),
     )
     reach_count = -(-WIN // tok_rows)
     earlier_blocks = []

time: 1480 us -> 1420 us (0.959)
  blocking collectives: 256 us -> 183 us
    all_gather x1 -> x0, blocking collectives: 77.9 us -> none  [body(): lax.all_gather(w_down, 'seq', axis=1, tiled=True)]
    psum x1, waiting for transfers between devices: 504 us -> 523 us  [body(): summed = lax.psum(stacked, 'seq')]
  transfers between devices with their start and end apart: 18 -> 19, of which waited for: 7 -> 7; matrix products, arithmetic and copies ran while one was open for 2% -> 3% of each run, Pallas kernels for 0% -> 0%
where the time goes in v1:
time: 1420 us
  waiting for transfers between devices  1090 us (77%)
  blocking collectives  183 us (13%)
  starting transfers between devices  74.8 us (5%)
  local copies, waits for them, and re-layouts  25.1 us (2%)
  matrix products  21.6 us (2%)
  between operations  14.9 us (1%)
    psum x1, waiting for transfers between devices, spread(): return lax.psum(block, axis)  555 us
    psum x1, waiting for transfers between devices, body(): summed = lax.psum(stacked, 'seq')  523 us
    all_gather x1, blocking collectives, body(): lax.all_gather(w_gate, 'seq', axis=1, tiled=True)  95.8 us
    all_gather x1, blocking collectives, body(): lax.all_gather(w_up, 'seq', axis=1, tiled=True)  77.9 us
    ppermute x16, starting transfers between devices, shifted(): lax.ppermute(array, axis, [(i, (i + by) % count) for i in range(count)])  66.6 us
  transfers between devices with their start and end apart: 19, of which 7 were waited for; matrix products, arithmetic and copies ran while one was open for 3% of the time, Pallas kernels for 0%

profile of v1, /device:TPU:1, one launch (start us, length us, event | category | flops | bytes accessed | tf_op | source)
XLA Modules:
  0.0 1420.5 jit_solution(10936810479203637554)
XLA Ops:
  6.5 11.6 collective-permute-start
  18.1 2.5 collective-permute-start.1
  20.6 6.6 collective-permute-start.2
  27.2 5.8 collective-permute-start.3
  33.0 4.0 collective-permute-start.4
  37.1 1.5 stack.37
  38.6 8.1 all-to-all-start
  47.3 95.8 %all_gather.6 = bf16[2,256,512]{2,0,1:T(2,128)(2,1)S(1)} all-gather(bf16[2,4,512]{2,0,1:T(2,128)(2,1)S(1)} %copy.87), channel_id=1, replica_groups=mesh['head'=8,'seq'=64] {'seq'}, dimensions={1}, use_global_device_ids=true | all-gather | bytes 532480 | tf_op jit(solution)/shard_map/all_gather | solution.py:75
  143.7 77.9 %all_gather.7 = bf16[2,256,512]{2,0,1:T(2,128)(2,1)S(1)} all-gather(bf16[2,4,512]{2,0,1:T(2,128)(2,1)S(1)} %copy.89), channel_id=1, replica_groups=mesh['head'=8,'seq'=64] {'seq'}, dimensions={1}, use_global_device_ids=true | all-gather | bytes 532480 | tf_op jit(solution)/shard_map/all_gather | solution.py:76
  223.6 1.0 fusion.51
  224.6 1.0 fusion.73
  227.1 2.0 copy.99
  230.0 1.9 collective-permute-start.5
  231.9 1.9 collective-permute-start.8
  233.9 1.9 collective-permute-start.9
  235.9 3.4 collective-permute-start.10
  239.3 9.6 collective-permute-start.11
  248.9 7.3 collective-permute-start.12
  256.2 2.2 collective-permute-start.13
  259.1 0.8 slice.109
  261.7 0.8 slice.112
  262.5 0.8 slice.113
  263.4 1.2 collective-permute-done.9
  264.6 1.9 collective-permute-start.6
  266.5 4.1 collective-permute-done.10
  270.6 1.9 collective-permute-start.14
  272.5 3.6 collective-permute-done.11
  276.1 1.9 collective-permute-start.15
  278.6 2.1 collective-permute-start.7
  280.7 0.9 collective-permute-done.13
  285.3 1.0 copy-done.17
  287.0 523.0 %all-reduce.20.cloned.1.call-done = f32[6,256,512]{2,1,0:T(8,128)} async-done(((f32[6,256,512]{2,1,0:T(8,128)}), f32[6,256,512]{2,1,0:T(8,128)}) %all-reduce.20.cloned.1.call-update) | async-done | bytes 3145744 | tf_op jit(solution)/shard_map/psum | solution.py:161
  810.0 1.8 multiply_reduce_fusion
  812.4 1.8 fusion.38
  814.6 1.9 convolution_add_fusion.4
  822.5 1.9 select_bitcast_fusion
  824.4 0.9 copy-done.5
  829.5 1.8 fusion.4
  832.9 554.7 %all-reduce.22.cloned.1.call-done = (bf16[1,256,512]{2,1,0:T(8,128)(2,1)}, bf16[1,256,512]{2,1,0:T(8,128)(2,1)}, bf16[1,256,512]{2,1,0:T(8,128)(2,1)}, bf16[1,25...) async-done(((bf16[1,256,512]{2,1,0:T(8,128)(2,1)}, bf16[1,256,512]{2,1,0:T(8,128)(2,1)}, bf16[1,256,512]{2,1,0:T(8,128)(2,1)}, ...) | async-done | bytes 1572880 | tf_op jit(solution)/shard_map/psum | solution.py:15
  1387.5 1.0 constant_dynamic-update-slice_fusion.5
  1388.6 1.0 constant_dynamic-update-slice_fusion.4
  1389.8 1.8 fusion.87
  1391.5 1.6 copy.121
  1393.1 2.6 copy.122
  1395.7 2.5 copy.123
  1398.5 2.1 convolution_bitcast_fusion.3
  1400.6 2.2 fusion.24
  1403.1 9.4 all_to_all.14
  (147 shorter events, 26.5 us)
Async XLA Ops:
  6.5 40.3 %copy-start.1 = (bf16[2,64,512]{2,1,0:T(8,128)(2,1)S(1)}, bf16[2,64,512]{2,1,0:T(8,128)(2,1)}, u32[]{:S(2)}) copy-start(bf16[2,64,512]{2,1,0:T(8,128)(2,1)} %param.10) | copy-start | bytes 393220
  6.5 222.8 %collective-permute-start = (bf16[2,64,512]{2,1,0:T(8,128)(2,1)}, bf16[2,64,512]{2,1,0:T(8,128)(2,1)}, u32[]{:S(2)}, u32[]{:S(2)}) collective-permute-start(bf16[2,64,512]{2,1,0:T(8,128)(2,1)} %param.11), channel_id=1, source_target_pairs={{0,8},{1,9},{2,10},{3,11},{4,12},{5,13},{6,14},{7,15},{8,16},{9,17... | collective-permute-start | bytes 393224 | tf_op jit(solution)/shard_map/ppermute | solution.py:20
  18.1 213.8 %collective-permute-start.1 = (bf16[2,64,512]{2,1,0:T(8,128)(2,1)}, bf16[2,64,512]{2,1,0:T(8,128)(2,1)}, u32[]{:S(2)}, u32[]{:S(2)}) collective-permute-start(bf16[2,64,512]{2,1,0:T(8,128)(2,1)} %param.11), channel_id=1, source_target_pairs={{0,7},{1,8},{2,9},{3,10},{4,11},{5,12},{6,13},{7,14},{8,15},{9,16}... | collective-permute-start | bytes 393224 | tf_op jit(solution)/shard_map/ppermute | solution.py:20
  20.6 213.3 %collective-permute-start.2 = (bf16[2,64,512]{2,1,0:T(8,128)(2,1)}, bf16[2,64,512]{2,1,0:T(8,128)(2,1)}, u32[]{:S(2)}, u32[]{:S(2)}) collective-permute-start(bf16[2,64,512]{2,1,0:T(8,128)(2,1)} %param.11), channel_id=1, source_target_pairs={{0,6},{1,7},{2,8},{3,9},{4,10},{5,11},{6,12},{7,13},{8,14},{9,15},... | collective-permute-start | bytes 393224 | tf_op jit(solution)/shard_map/ppermute | solution.py:20
  27.2 208.7 %collective-permute-start.3 = (bf16[2,64,512]{2,1,0:T(8,128)(2,1)}, bf16[2,64,512]{2,1,0:T(8,128)(2,1)}, u32[]{:S(2)}, u32[]{:S(2)}) collective-permute-start(bf16[2,64,512]{2,1,0:T(8,128)(2,1)} %param.11), channel_id=1, source_target_pairs={{0,5},{1,6},{2,7},{3,8},{4,9},{5,10},{6,11},{7,12},{8,13},{9,14},{... | collective-permute-start | bytes 393224 | tf_op jit(solution)/shard_map/ppermute | solution.py:20
  33.0 206.2 %collective-permute-start.4 = (bf16[2,64,512]{2,1,0:T(8,128)(2,1)}, bf16[2,64,512]{2,1,0:T(8,128)(2,1)}, u32[]{:S(2)}, u32[]{:S(2)}) collective-permute-start(bf16[2,64,512]{2,1,0:T(8,128)(2,1)} %param.11), channel_id=1, source_target_pairs={{0,4},{1,5},{2,6},{3,7},{4,8},{5,9},{6,10},{7,11},{8,12},{9,13},{1... | collective-permute-start | bytes 393224 | tf_op jit(solution)/shard_map/ppermute | solution.py:20
  38.6 8.7 copy-start.18
  38.6 187.1 %all-to-all-start = ((bf16[64,2,8,256]{3,2,1,0:T(8,128)(2,1)}), bf16[64,2,8,256]{3,2,1,0:T(8,128)(2,1)S(1)}, u32[]{:S(2)}, u32[]{:S(2)}) async-start(bf16[64,2,8,256]{3,2,1,0:T(8,128)(2,1)} %stack.37), calls=%async_computation | async-start | bytes 1048576 | tf_op jit(solution)/shard_map/all_to_all | solution.py:72
  46.7 763.2 %all-reduce.20.cloned.1.call-start = ((), (), s32[]{:S(2)}) async-start(), calls=%async_computation.2 | async-start | bytes 6291456 | tf_op jit(solution)/shard_map/psum | solution.py:161
  46.8 96.8 %copy-start.19 = (bf16[2,4,512]{2,1,0:T(4,128)(2,1)S(1)}, bf16[2,4,512]{2,1,0:T(4,128)(2,1)}, u32[]{:S(2)}) copy-start(bf16[2,4,512]{2,1,0:T(4,128)(2,1)} %param.15) | copy-start | bytes 24580
  222.2 0.9 copy-start.8
  222.2 1.0 copy-start.2
  222.2 1.1 copy-start.21
  229.1 0.9 copy-start.9
  229.1 1158.4 %all-reduce.22.cloned.1.call-start = ((), (), s32[]{:S(2)}) async-start(), calls=%async_computation.3 | async-start | bytes 3145728 | tf_op jit(solution)/shard_map/psum | solution.py:15
  230.0 18.9 %collective-permute-start.5 = (bf16[2,64,512]{2,1,0:T(8,128)(2,1)S(1)}, bf16[2,64,512]{2,1,0:T(8,128)(2,1)S(1)}, u32[]{:S(2)}, u32[]{:S(2)}) collective-permute-start(bf16[2,64,512]{2,1,0:T(8,128)(2,1)S(1)} %copy-done.9), channel_id=1, source_target_pairs={{0,3},{1,4},{2,5},{3,6},{4,7},{5,8},{6,9},{7,10},{8,11},{9,12},{10... | collective-permute-start | bytes 393224 | tf_op jit(solution)/shard_map/ppermute | solution.py:20
  231.9 24.3 %collective-permute-start.8 = (bf16[2,64,512]{2,1,0:T(8,128)(2,1)S(1)}, bf16[2,64,512]{2,1,0:T(8,128)(2,1)S(1)}, u32[]{:S(2)}, u32[]{:S(2)}) collective-permute-start(bf16[2,64,512]{2,1,0:T(8,128)(2,1)S(1)} %copy-done.1), channel_id=1, source_target_pairs={{0,8},{1,9},{2,10},{3,11},{4,12},{5,13},{6,14},{7,15},{8,16},{9,17... | collective-permute-start | bytes 393224 | tf_op jit(solution)/shard_map/ppermute | solution.py:20
  233.9 30.6 %collective-permute-start.9 = (bf16[2,64,512]{2,1,0:T(8,128)(2,1)S(1)}, bf16[2,64,512]{2,1,0:T(8,128)(2,1)S(1)}, u32[]{:S(2)}, u32[]{:S(2)}) collective-permute-start(bf16[2,64,512]{2,1,0:T(8,128)(2,1)S(1)} %copy-done.1), channel_id=1, source_target_pairs={{0,7},{1,8},{2,9},{3,10},{4,11},{5,12},{6,13},{7,14},{8,15},{9,16}... | collective-permute-start | bytes 393224 | tf_op jit(solution)/shard_map/ppermute | solution.py:20
  235.9 34.7 %collective-permute-start.10 = (bf16[2,64,512]{2,1,0:T(8,128)(2,1)S(1)}, bf16[2,64,512]{2,1,0:T(8,128)(2,1)S(1)}, u32[]{:S(2)}, u32[]{:S(2)}) collective-permute-start(bf16[2,64,512]{2,1,0:T(8,128)(2,1)S(1)} %copy-done.1), channel_id=1, source_target_pairs={{0,6},{1,7},{2,8},{3,9},{4,10},{5,11},{6,12},{7,13},{8,14},{9,15},... | collective-permute-start | bytes 393224 | tf_op jit(solution)/shard_map/ppermute | solution.py:20
  239.3 36.8 %collective-permute-start.11 = (bf16[2,64,512]{2,1,0:T(8,128)(2,1)S(1)}, bf16[2,64,512]{2,1,0:T(8,128)(2,1)S(1)}, u32[]{:S(2)}, u32[]{:S(2)}) collective-permute-start(bf16[2,64,512]{2,1,0:T(8,128)(2,1)S(1)} %copy-done.1), channel_id=1, source_target_pairs={{0,5},{1,6},{2,7},{3,8},{4,9},{5,10},{6,11},{7,12},{8,13},{9,14},{... | collective-permute-start | bytes 393224 | tf_op jit(solution)/shard_map/ppermute | solution.py:20
  248.9 34.1 %copy-start.6 = (bf16[2,64,512]{2,1,0:T(8,128)(2,1)}, bf16[2,64,512]{2,1,0:T(8,128)(2,1)S(1)}, u32[]{:S(2)}) copy-start(bf16[2,64,512]{2,1,0:T(8,128)(2,1)S(1)} %collective-permute-done.5) | copy-start | bytes 393220
  248.9 29.7 %collective-permute-start.12 = (bf16[2,64,512]{2,1,0:T(8,128)(2,1)S(1)}, bf16[2,64,512]{2,1,0:T(8,128)(2,1)S(1)}, u32[]{:S(2)}, u32[]{:S(2)}) collective-permute-start(bf16[2,64,512]{2,1,0:T(8,128)(2,1)S(1)} %copy-done.1), channel_id=1, source_target_pairs={{0,4},{1,5},{2,6},{3,7},{4,8},{5,9},{6,10},{7,11},{8,12},{9,13},{1... | collective-permute-start | bytes 393224 | tf_op jit(solution)/shard_map/ppermute | solution.py:20
  256.2 25.4 %collective-permute-start.13 = (bf16[2,64,512]{2,1,0:T(8,128)(2,1)S(1)}, bf16[2,64,512]{2,1,0:T(8,128)(2,1)S(1)}, u32[]{:S(2)}, u32[]{:S(2)}) collective-permute-start(bf16[2,64,512]{2,1,0:T(8,128)(2,1)S(1)} %copy-done.1), channel_id=1, source_target_pairs={{0,3},{1,4},{2,5},{3,6},{4,7},{5,8},{6,9},{7,10},{8,11},{9,12},{10... | collective-permute-start | bytes 393224 | tf_op jit(solution)/shard_map/ppermute | solution.py:20
  264.6 561.4 %collective-permute-start.6 = (bf16[2,64,512]{2,1,0:T(8,128)(2,1)S(1)}, bf16[2,64,512]{2,1,0:T(8,128)(2,1)S(1)}, u32[]{:S(2)}, u32[]{:S(2)}) collective-permute-start(bf16[2,64,512]{2,1,0:T(8,128)(2,1)S(1)} %copy-done.9), channel_id=1, source_target_pairs={{0,2},{1,3},{2,4},{3,5},{4,6},{5,7},{6,8},{7,9},{8,10},{9,11},{10,... | collective-permute-start | bytes 393224 | tf_op jit(solution)/shard_map/ppermute | solution.py:20
  270.6 555.4 %collective-permute-start.14 = (bf16[2,64,512]{2,1,0:T(8,128)(2,1)S(1)}, bf16[2,64,512]{2,1,0:T(8,128)(2,1)S(1)}, u32[]{:S(2)}, u32[]{:S(2)}) collective-permute-start(bf16[2,64,512]{2,1,0:T(8,128)(2,1)S(1)} %copy-done.1), channel_id=1, source_target_pairs={{0,2},{1,3},{2,4},{3,5},{4,6},{5,7},{6,8},{7,9},{8,10},{9,11},{10,... | collective-permute-start | bytes 393224 | tf_op jit(solution)/shard_map/ppermute | solution.py:20
  276.1 549.9 %collective-permute-start.15 = (bf16[2,64,512]{2,1,0:T(8,128)(2,1)S(1)}, bf16[2,64,512]{2,1,0:T(8,128)(2,1)S(1)}, u32[]{:S(2)}, u32[]{:S(2)}) collective-permute-start(bf16[2,64,512]{2,1,0:T(8,128)(2,1)S(1)} %copy-done.1), channel_id=1, source_target_pairs={{0,1},{1,2},{2,3},{3,4},{4,5},{5,6},{6,7},{7,8},{8,9},{9,10},{10,1... | collective-permute-start | bytes 393224 | tf_op jit(solution)/shard_map/ppermute | solution.py:20
  278.6 547.4 %collective-permute-start.7 = (bf16[2,64,512]{2,1,0:T(8,128)(2,1)S(1)}, bf16[2,64,512]{2,1,0:T(8,128)(2,1)S(1)}, u32[]{:S(2)}, u32[]{:S(2)}) collective-permute-start(bf16[2,64,512]{2,1,0:T(8,128)(2,1)S(1)} %copy-done.9), channel_id=1, source_target_pairs={{0,1},{1,2},{2,3},{3,4},{4,5},{5,6},{6,7},{7,8},{8,9},{9,10},{10,1... | collective-permute-start | bytes 393224 | tf_op jit(solution)/shard_map/ppermute | solution.py:20
  281.6 2.9 copy-start.4
  283.1 3.2 copy-start.7
  283.1 3.2 slice-start.1
  285.3 1.0 copy-start.17
  824.4 0.9 copy-start.5
  824.4 0.9 slice-start
  826.0 3.5 copy-start.3
  826.0 3.5 copy-start.15
  829.5 2.9 copy-start.10
  831.3 0.8 copy-start
  1387.5 2.1 copy-start.14
  1387.5 2.1 copy-start.13
  1387.5 2.1 copy-start.12
  1388.6 1.1 copy-start.11
  1395.6 2.5 copy-start.20
  1402.8 10.1 copy-start.16
Sparse Core Ops, SparseCore 0:
  229.2 580.6 all-reduce.19
  824.5 562.9 all-reduce.21
